TPU v7x, 256 devices: a whole 4x4x8 slice. The times are simulated.
256 devices in a mesh: tok: 32 (over y, z), voc: 8 (over x, core).
Axes of the slice: x: 4, y: 4, z: 8, core: 2. Of those that a mesh axis runs over, the one named last changes fastest.
Arguments:
- teacher_rows: bfloat16 [8192, 2048], P('tok', 'voc')
- drafter_rows: bfloat16 [8192, 2048], P('tok', 'voc')
- head: bfloat16 [2048, 16384], P(None, 'voc'), may hold values from -1 to 1
- fr_ids: int32 [16384], P('voc'), may hold values from 0 to 151935, as said below
- targets: int32 [8192], P('tok'), may hold values from 0 to 151935
- dest_index: int32 [8192], P('tok'), may hold values from -1 to 8191, as said below
- counts: int32 [32], replicated, may hold values from 64 to 256, as said below
Outputs:
- row_loss: float32 [8192], P('tok')
- drafter_grad: bfloat16 [8192, 2048], P('tok', 'voc')
Inputs may be any that keep to these rules, and one draw needn't show every extreme that they name: `dest_index`: the prefill rows that name a slot name distinct slots. With blocks of 256 rows and 32 blocks, a row of prefill block b names a slot of drafter block (b + k) mod 32 for k in 0, 1, 16, 17; at most 64 rows go from one prefill block to one drafter block, and every drafter block receives exactly 64 from its own prefill block. The slots named in drafter block j are exactly its first counts[j] slots, grouped by k in that order. counts[j] is the number of prefill rows that name a slot of block j; some block is full. `fr_ids`: distinct ids.
All inputs are finite; a program needn't handle non-finite values.
Results may differ from a plain program's by a relative error of at most 0.0041.
Values may be sent and summed in bfloat16 or wider, within the bound.
A program may use at most 64 MiB of HBM per device.

v0:
```python
import jax
import jax.numpy as jnp
from jax import lax
from jax.sharding import PartitionSpec as P

loss_scale = 16.0


def encode(values):
    return jnp.stack([values // 128, values % 128], axis=1).astype(jnp.float32).astype(jnp.bfloat16)


def decode(code):
    widened = code.astype(jnp.float32)
    return (widened[:, 0] * 128.0 + widened[:, 1]).astype(jnp.int32)


def per_device(teacher_rows, drafter_rows, head, fr_ids, targets, dest_index, counts):
    row_count = teacher_rows.shape[0]
    tok_index = lax.axis_index("tok")
    first_slot = tok_index * row_count
    slot_ids = jnp.arange(row_count, dtype=jnp.int32)
    code = encode(dest_index + 1)
    rows_piece = lax.all_gather(teacher_rows, "tok", axis=0, tiled=True)
    code_piece = lax.all_gather(code, "tok", axis=0, tiled=True)
    wanted = decode(code_piece) - 1 - first_slot
    select = (slot_ids[:, None] == wanted[None, :]).astype(jnp.bfloat16)
    moved = jnp.dot(select, rows_piece, preferred_element_type=jnp.float32).astype(jnp.bfloat16)
    teacher_full, drafter_full = (
        lax.all_gather(moved, "voc", axis=1, tiled=True),
        lax.all_gather(drafter_rows, "voc", axis=1, tiled=True),
    )
    teach_logit = jnp.dot(teacher_full, head, preferred_element_type=jnp.float32)
    draft_logit = jnp.dot(drafter_full, head, preferred_element_type=jnp.float32)
    hit_table = (targets[:, None] == fr_ids[None, :]).astype(jnp.float32)
    local_hits = jnp.sum(hit_table, axis=1)
    local_target = jnp.sum(hit_table * draft_logit, axis=1)
    teach_max, draft_max = lax.pmax(
        (jnp.max(teach_logit, axis=1), jnp.max(draft_logit, axis=1)), "voc"
    )
    teach_exp = jnp.exp(teach_logit - teach_max[:, None])
    draft_exp = jnp.exp(draft_logit - draft_max[:, None])
    teach_total, draft_total, cross, target_logit, hits = lax.psum(
        (
            jnp.sum(teach_exp, axis=1),
            jnp.sum(draft_exp, axis=1),
            jnp.sum(teach_exp * (teach_logit - draft_logit), axis=1),
            local_target,
            local_hits,
        ),
        "voc",
    )
    valid = (slot_ids < counts[tok_index]).astype(jnp.float32)
    teach_lse = teach_max + jnp.log(teach_total)
    draft_lse = draft_max + jnp.log(draft_total)
    row_loss = valid * (
        cross / teach_total - teach_lse + draft_lse + hits * (draft_lse - target_logit)
    )
    teach_prob = teach_exp / teach_total[:, None]
    draft_prob = draft_exp / draft_total[:, None]
    grad_logit = (
        valid[:, None] * ((1.0 + hits)[:, None] * draft_prob - teach_prob - hit_table)
    ).astype(jnp.bfloat16)
    summed = lax.psum_scatter(
        lax.dot_general(
            head, grad_logit, (((1,), (1,)), ((), ())), preferred_element_type=jnp.float32
        ),
        "voc",
        scatter_dimension=0,
        tiled=True,
    )
    drafter_grad = (loss_scale * summed).T.astype(jnp.bfloat16)
    return (row_loss, drafter_grad)


def solution(mesh):
    return jax.shard_map(
        per_device,
        mesh=mesh,
        in_specs=(
            P("tok", "voc"),
            P("tok", "voc"),
            P(None, "voc"),
            P("voc"),
            P("tok"),
            P("tok"),
            P(),
        ),
        out_specs=(P("tok"), P("tok", "voc")),
        check_vma=False,
    )
```

profile of v0, /device:TPU:1, one launch (start us, length us, event | category | flops | bytes accessed | tf_op | source)
XLA Modules:
  0.0 238.1 jit_solution(6944104512413968319)
XLA Ops:
  7.2 0.0 all-gather.4.cloned.1.call-start
  7.2 0.7 all-gather.4.cloned.1.call-update
  7.9 0.0 all-gather.8.cloned.1.call-start
  7.9 0.7 all-gather.8.cloned.1.call-update
  8.6 0.0 all-gather.6.cloned.1.call-start
  8.7 0.7 and_select_fusion.1
  9.4 37.7 %all_gather.12 = bf16[8192,2]{0,1:T(2,128)(2,1)S(1)} all-gather(bf16[256,2]{0,1:T(2,128)(2,1)S(1)} %fusion.21), channel_id=1, replica_groups=mesh['tok'=32,'voc'=8] {'tok'}, dimensions={0}, use_global_device_ids=true | all-gather | bytes 33792 | tf_op jit(solution)/shard_map/all_gather | solution.py:25
  47.1 0.1 fusion.20
  47.2 46.4 %all-gather.4.cloned.1.call-done = bf16[8192,256]{1,0:T(8,128)(2,1)} async-done(((bf16[256,256]{1,0:T(8,128)(2,1)}), bf16[8192,256]{1,0:T(8,128)(2,1)}) %all-gather.4.cloned.1.call-update) | async-done | bytes 4194320 | tf_op jit(solution)/shard_map/all_gather | solution.py:24
  93.6 4.1 %fusion.7 = bf16[256,256]{1,0:T(8,128)(2,1)} fusion(bf16[8192,256]{1,0:T(8,128)(2,1)} %all-gather.4.cloned.1.call-done, s32[8192]{0:T(1024)S(1)} %bitcast.14), kind=kOutput, calls=%fused_computation.15 | convolution fusion | flops 1075904512 | bytes 4358144 | tf_op jit(solution)/shard_map/dot_general | solution.py:28
  97.7 0.0 reduce-scatter.2.cloned.1.call-start
  97.8 0.6 dynamic_slice.3
  98.4 0.5 fusion.22
  98.9 22.7 %all-gather.8.cloned.1.call-done = bf16[256,2048]{1,0:T(8,128)(2,1)} async-done(((bf16[256,256]{1,0:T(8,128)(2,1)}), bf16[256,2048]{1,0:T(8,128)(2,1)}) %all-gather.8.cloned.1.call-update) | async-done | bytes 1048592 | tf_op jit(solution)/shard_map/all_gather | solution.py:31
  121.6 6.1 %fusion.24 = (f32[256]{0:T(256)S(1)}, f32[256,2048]{1,0:T(8,128)S(1)}) fusion(bf16[256,2048]{1,0:T(8,128)(2,1)} %all-gather.8.cloned.1.call-done, bf16[2048,2048]{1,0:T(8,128)(2,1)} %param.9), kind=kOutput, calls=%fused_computation.45 | convolution fusion | flops 2148007680 | bytes 11535360 | tf_op jit(solution)/shard_map/dot_general | solution.py:34
  127.8 23.2 %all-gather.6.cloned.1.call-done = bf16[256,2048]{1,0:T(8,128)(2,1)} async-done(((bf16[256,256]{1,0:T(8,128)(2,1)}), bf16[256,2048]{1,0:T(8,128)(2,1)}) %all-gather.6.cloned.1.call-update) | async-done | bytes 1048592 | tf_op jit(solution)/shard_map/all_gather | solution.py:30
  151.0 7.4 %fusion.23 = (f32[256]{0:T(256)S(1)}, f32[256,2048]{1,0:T(8,128)}) fusion(bf16[256,2048]{1,0:T(8,128)(2,1)} %all-gather.6.cloned.1.call-done, bf16[2048,2048]{1,0:T(8,128)(2,1)} %param.9), kind=kOutput, calls=%fused_computation.44 | convolution fusion | flops 2148007680 | bytes 11535360 | tf_op jit(solution)/shard_map/dot_general | solution.py:33
  158.4 12.0 %all-reduce.1 = (f32[256]{0:T(256)S(1)}, f32[256]{0:T(256)S(1)}) all-reduce(f32[256]{0:T(256)S(1)} %get-tuple-element.18, f32[256]{0:T(256)S(1)} %get-tuple-element.20), channel_id=1, replica_groups=mesh['tok'=32,'voc'=8] {'voc'}, use_global_device_ids=true, to_apply=%region_1.2 | all-reduce | flops 512 | bytes 4096 | tf_op jit(solution)/shard_map/pmax | solution.py:38
  170.4 3.0 %multiply_reduce_fusion = (f32[256]{0:T(256)S(1)}, f32[256]{0:T(256)S(1)}, f32[256]{0:T(256)S(1)}, f32[256]{0:T(256)S(1)}, f32[256]{0:T(256)S(1)}) fusion(f32[256,2048]{1,0:T(8,128)} %get-tuple-element.19, f32[256,2048]{1,0:T(8,128)S(1)} %get-tuple-element.21, f32[256]{0:T(256)S(1)} %get-tuple-element.12, s32[2048]{0:T(1024)S(1)} %copy-done, ...), kind=kLoop, calls=%fused_computation.11 | loop fusion | flops 6290176 | bytes 4210688 | tf_op jit(solution)/shard_map/reduce_sum | solution.py:47
  173.5 14.5 %all-reduce = (f32[256]{0:T(256)S(1)}, f32[256]{0:T(256)S(1)}, f32[256]{0:T(256)S(1)}, f32[256]{0:T(256)S(1)}, f32[256]{0:T(256)S(1)}) all-reduce(f32[256]{0:T(256)S(1)} %get-tuple-element.6, f32[256]{0:T(256)S(1)} %get-tuple-element.4, f32[256]{0:T(256)S(1)} %get-tuple-element.5, ...), channel_id=1, replica_groups=mesh['tok'=32,'voc'=8] {'voc'}, use_global_device_ids=true, to_apply=%region_11.12 | all-reduce | flops 1280 | bytes 10240 | tf_op jit(solution)/shard_map/psum | solution.py:43
  188.0 1.1 broadcast_add_fusion
  189.1 8.3 %convolution_bitcast_fusion = f32[2048,256]{0,1:T(8,128)} fusion(bf16[2048,2048]{1,0:T(8,128)(2,1)} %param.9, f32[256,2048]{1,0:T(8,128)} %get-tuple-element.19, f32[256,2048]{1,0:T(8,128)S(1)} %get-tuple-element.21, f32[256]{0:T(256)S(1)} %get-tuple-element.10, f32[256]{0:T(256)S(1)} %get-tuple-element.9, f32[256]{0:T(256)S(1)} %get-tuple-element.14, ...), kind=kOutput, calls=%fused_computation.6 | convolution fusion | flops 2153250816 | bytes 14695424 | tf_op jit(solution)/shard_map/dot_general | solution.py:65
  197.4 32.6 %reduce-scatter.2.cloned.1.call-done = f32[256,256]{0,1:T(8,128)} async-done(((f32[2048,256]{0,1:T(8,128)}), f32[256,256]{0,1:T(8,128)}) %reduce-scatter.2.cloned.1.call-update) | async-done | bytes 262160 | tf_op jit(solution)/shard_map/reduce_scatter | solution.py:64
  230.0 1.6 fusion.17
  (10 shorter events, 0.1 us)
Async XLA Ops:
  7.2 86.4 %all-gather.4.cloned.1.call-start = ((), (), s32[]{:S(2)}) async-start(), calls=%async_computation.1 | async-start | bytes 4325376 | tf_op jit(solution)/shard_map/all_gather | solution.py:24
  7.9 113.7 %all-gather.8.cloned.1.call-start = ((), (), s32[]{:S(2)}) async-start(), calls=%async_computation.3 | async-start | bytes 1179648 | tf_op jit(solution)/shard_map/all_gather | solution.py:31
  8.6 142.3 %all-gather.6.cloned.1.call-start = ((), (), s32[]{:S(2)}) async-start(), calls=%async_computation.2 | async-start | bytes 1179648 | tf_op jit(solution)/shard_map/all_gather | solution.py:30
  93.6 4.2 %copy-start.2 = (s32[32]{0:T(128)S(1)}, s32[32]{0:T(128)}, u32[]{:S(2)}) copy-start(s32[32]{0:T(128)} %param.13) | copy-start | bytes 388
  97.7 132.2 %reduce-scatter.2.cloned.1.call-start = ((), (), s32[]{:S(2)}) async-start(), calls=%async_computation.4 | async-start | bytes 2359296 | tf_op jit(solution)/shard_map/reduce_scatter | solution.py:64
  127.8 42.6 %copy-start = (s32[2048]{0:T(1024)S(1)}, s32[2048]{0:T(1024)}, u32[]{:S(2)}) copy-start(s32[2048]{0:T(1024)} %param.10) | copy-start | bytes 24580
  127.8 42.6 %copy-start.1 = (s32[256]{0:T(256)S(1)}, s32[256]{0:T(256)}, u32[]{:S(2)}) copy-start(s32[256]{0:T(256)} %param.11) | copy-start | bytes 3076
Sparse Core Ops, SparseCore 0:
  10.6 82.9 all-gather.3
  95.4 26.1 all-gather.7
  124.0 26.8 all-gather.5
  197.5 32.4 reduce-scatter.1
where the time goes:
time: 240 us; the launch traced here: 238 us
  waiting for transfers between devices  126 us (52%)
  blocking collectives  64.2 us (27%)
  matrix products  25.9 us (11%)
  between operations  13.8 us (6%)
  other arithmetic  7.13 us (3%)
    all_gather x1, waiting for transfers between devices, per_device(): rows_piece = lax.all_gather(teacher_rows, 'tok', axis=0, tiled=True)  46.4 us
    all_gather x1, blocking collectives, per_device(): code_piece = lax.all_gather(code, 'tok', axis=0, tiled=True)  37.7 us
    reduce_scatter x1, waiting for transfers between devices, per_device(): lax.psum_scatter(lax.dot_general(head, grad_logit, (((1,), (1,)), ((), ()...  32.6 us
    all_gather x1, waiting for transfers between devices, per_device(): lax.all_gather(moved, 'voc', axis=1, tiled=True)  23.2 us
    all_gather x1, waiting for transfers between devices, per_device(): lax.all_gather(drafter_rows, 'voc', axis=1, tiled=True)  22.7 us
    psum x1, blocking collectives, per_device(): lax.psum((jnp.sum(teach_exp, axis=1), jnp.sum(draft_exp, axis=1), jnp.sum...  14.5 us
    pmax x1, blocking collectives, per_device(): lax.pmax((jnp.max(teach_logit, axis=1), jnp.max(draft_logit, axis=1)), 'v...  12 us
    dot_general x1, matrix products, per_device(): lax.dot_general(head, grad_logit, (((1,), (1,)), ((), ())), preferred_ele...  8.28 us
  transfers between devices with their start and end apart: 4, of which 4 were waited for; matrix products, arithmetic and copies ran while one was open for 5% of the time, Pallas kernels for 0%

commit v1 on v0

v1 whole, which is shorter than its diff:
```python
import functools

import jax
import jax.numpy as jnp
from jax import lax
from jax.experimental import pallas as pl
from jax.experimental.pallas import tpu as pltpu
from jax.sharding import PartitionSpec as P

loss_scale = 16.0
MESH = pl.DeviceIdType.MESH
NT = (((1,), (1,)), ((), ()))
F32 = jnp.float32
BF16 = jnp.bfloat16


def kernel(
    n_tok,
    teach,
    draft,
    head,
    fr,
    targ,
    dest,
    counts,
    loss,
    grad,
    head_v,
    head_t,
    rows_d,
    rows_t,
    teach_v,
    pack,
    got,
    tl,
    dl,
    ed,
    hit,
    g,
    part,
    sibp,
    two,
    far_l,
    far_r,
    near,
    in_l,
    in_r,
    stats,
    load_sem,
    ag_send,
    ag_recv,
    pk_send,
    pk_recv,
    st_send,
    st_recv,
    rs_send,
    rs_recv,
):
    n, r = hit.shape
    f = teach.shape[1]
    quarter = r // 4
    half = r // 2
    fh = f // 2
    shifts = (0, 1, n_tok // 2, n_tok // 2 + 1)
    t = lax.axis_index("tok")
    v = lax.axis_index("voc")
    x = lax.div(v, 2)
    c = lax.rem(v, 2)
    xr = lax.rem(x + 1, 4)
    xl = lax.rem(x + 3, 4)
    xo = lax.rem(x + 2, 4)
    sib = x * 2 + 1 - c
    right = xr * 2 + c
    left = xl * 2 + c
    opp = xo * 2 + c
    right_s = xr * 2 + 1 - c
    left_s = xl * 2 + 1 - c
    opp_s = xo * 2 + 1 - c

    barrier = pltpu.get_barrier_semaphore()
    greet = sorted({s % n_tok for k in shifts[1:] for s in (k, n_tok - k)})
    for k in greet:
        pl.semaphore_signal(
            barrier, inc=1, device_id={"tok": lax.rem(t + k, n_tok)}, device_id_type=MESH
        )
    for i in range(1, 8):
        pl.semaphore_signal(
            barrier, inc=1, device_id={"voc": lax.rem(v + i, 8)}, device_id_type=MESH
        )

    load_d = pltpu.make_async_copy(draft, rows_d.at[v], load_sem.at[0])
    load_t = pltpu.make_async_copy(teach, teach_v, load_sem.at[1])
    load_h = [
        pltpu.make_async_copy(
            head.at[pl.ds(i * 2 * f, 2 * f)], head_v.at[i], load_sem.at[2 + i]
        )
        for i in range(4)
    ]
    load_d.start()
    load_t.start()
    for cp in load_h:
        cp.start()

    def remote(src, dst, ssem, rsem, to):
        return pltpu.make_async_remote_copy(
            src_ref=src, dst_ref=dst, send_sem=ssem, recv_sem=rsem,
            device_id=to, device_id_type=MESH,
        )

    lo, hi = pl.ds(0, half), pl.ds(half, half)

    def gather(q, rows):
        def whole(i, p, to):
            return remote(
                rows.at[p], rows.at[p], ag_send.at[q, i], ag_recv.at[q, i], {"voc": to}
            )

        def halves(i, p, h, to):
            return remote(
                rows.at[p, h], rows.at[p, h], ag_send.at[q, i], ag_recv.at[q, i], {"voc": to}
            )

        send = [
            whole(0, v, sib),
            halves(1, v, lo, right),
            halves(2, v, hi, right),
            halves(3, v, hi, left),
            halves(4, v, lo, left),
            halves(5, left, lo, right),
            halves(6, right, hi, left),
            whole(7, left, sib),
            whole(8, right, sib),
            halves(9, opp, lo, sib),
            halves(10, opp, hi, sib),
        ]
        recv = [
            whole(0, sib, sib),
            halves(1, left, lo, right),
            halves(2, left, hi, right),
            halves(3, right, hi, left),
            halves(4, right, lo, left),
            halves(5, opp, lo, right),
            halves(6, opp, hi, left),
            whole(7, left_s, sib),
            whole(8, right_s, sib),
            halves(9, opp_s, lo, sib),
            halves(10, opp_s, hi, sib),
        ]
        return send, recv

    d_send, d_recv = gather(0, rows_d)
    t_send, t_recv = gather(1, rows_t)

    load_d.wait()
    pl.semaphore_wait(barrier, len(greet) + 7)
    for i in (1, 3, 2, 4, 0):
        d_send[i].start()

    load_t.wait()
    dest_row = dest[...]
    place = lax.rem(dest_row + r, quarter)
    spot = lax.broadcasted_iota(jnp.int32, (quarter, r), 0)
    picks = []
    sizes = []
    for k in shifts:
        rel = dest_row - lax.rem(t + k, n_tok) * r
        inside = (rel >= 0) & (rel < r)
        picks.append(jnp.where(jnp.where(inside, place, -1) == spot, 1.0, 0.0).astype(F32))
        sizes.append(jnp.sum(jnp.where(inside, 1.0, 0.0).astype(F32), axis=1, keepdims=True))
    picked = jnp.dot(
        jnp.concatenate(picks, axis=0).astype(BF16), teach_v[...], preferred_element_type=F32
    ).astype(BF16)
    for i in range(4):
        pack[i, 0:quarter, :] = picked[i * quarter : (i + 1) * quarter, :]
        pack[i, quarter : quarter + 16, :] = jnp.broadcast_to(sizes[i], (16, f)).astype(BF16)
    repack = [
        remote(
            pack.at[i], got.at[i], pk_send.at[i], pk_recv.at[i],
            {"tok": lax.rem(t + shifts[i], n_tok)},
        )
        for i in range(1, 4)
    ]
    for cp in repack:
        cp.start()

    targets = targ[...].astype(F32)
    hits_sum = jnp.zeros((8, r), F32)
    for j in range(n // 128):
        ids = fr[0:1, j * 128 : (j + 1) * 128].astype(F32)
        ids = jnp.broadcast_to(ids, (128, 128)).T
        ids = jnp.concatenate([ids] * (r // 128), axis=1) if r >= 128 else ids[:, :r]
        h = jnp.where(ids == targets, 1.0, 0.0).astype(F32)
        hit[j * 128 : (j + 1) * 128, :] = h
        hits_sum = hits_sum + jnp.sum(h.reshape(16, 8, r), axis=0)
    local_hits = jnp.sum(hits_sum, axis=0, keepdims=True)

    def turn(i):
        load_h[i].wait()
        for b in range(2):
            for j in range(n // 256):
                head_t[2 * i + b, j * 256 : (j + 1) * 256, :] = head_v[
                    i, b * f : (b + 1) * f, j * 256 : (j + 1) * 256
                ].T

    turn(0)
    for cp in repack:
        cp.wait_recv()
    one = [got[i, quarter : quarter + 1, :].astype(F32) for i in range(1, 4)]
    start = [jnp.full((1, f), float(quarter), F32)]
    for i in range(2):
        start.append(start[-1] + one[i])
    rows_t[v, 0:quarter, :] = pack[0, 0:quarter, :]
    for q in range(1, 4):
        slot = lax.broadcasted_iota(jnp.int32, (quarter, f), 0).astype(F32) + float(q * quarter)
        total = jnp.zeros((quarter, f), F32)
        for i in range(3):
            mine = (slot >= start[i]) & (slot < start[i] + one[i])
            total = total + jnp.where(mine, got[i + 1, 0:quarter, :].astype(F32), 0.0)
        rows_t[v, q * quarter : (q + 1) * quarter, :] = total.astype(BF16)
    for i in (1, 3, 2, 4, 0):
        t_send[i].start()

    turn(1)
    d_recv[1].wait_recv()
    d_send[5].start()
    d_recv[3].wait_recv()
    d_send[6].start()
    turn(2)
    d_recv[2].wait_recv()
    d_send[7].start()
    d_recv[4].wait_recv()
    d_send[8].start()
    turn(3)

    tb = min(n, 512)

    def multiply(acc, rows, ks, first):
        def body(j, carry):
            sl = pl.ds(pl.multiple_of(j * tb, tb), tb)
            s = None
            for k in ks:
                d = lax.dot_general(head_t[k, sl, :], rows[k], NT, preferred_element_type=F32)
                s = d if s is None else s + d
            if not first:
                s = s + acc[sl, :]
            acc[sl, :] = s
            return carry

        lax.fori_loop(0, n // tb, body, 0)

    sb = min(n, 256)

    def fold(a, op):
        return op(a.reshape(sb // 8, 8, r), axis=0)

    def row_max(acc):
        def body(j, m):
            sl = pl.ds(pl.multiple_of(j * sb, sb), sb)
            return jnp.maximum(m, fold(acc[sl, :], jnp.max))

        m = lax.fori_loop(0, n // sb, body, jnp.full((8, r), -jnp.inf, F32))
        return jnp.max(m, axis=0, keepdims=True)

    d_recv[0].wait_recv()
    multiply(dl, rows_d, (v, sib), True)
    multiply(dl, rows_d, (left, right), False)
    d_recv[5].wait_recv()
    d_send[9].start()
    d_recv[6].wait_recv()
    d_send[10].start()
    t_recv[1].wait_recv()
    t_send[5].start()
    t_recv[3].wait_recv()
    t_send[6].start()
    d_recv[7].wait_recv()
    d_recv[8].wait_recv()
    multiply(dl, rows_d, (left_s, right_s), False)
    t_recv[2].wait_recv()
    t_send[7].start()
    t_recv[4].wait_recv()
    t_send[8].start()
    d_recv[9].wait_recv()
    d_recv[10].wait_recv()
    multiply(dl, rows_d, (opp, opp_s), False)

    draft_max = row_max(dl)

    def draft_body(j, carry):
        total, wanted = carry
        sl = pl.ds(pl.multiple_of(j * sb, sb), sb)
        d = dl[sl, :]
        e = jnp.exp(d - draft_max)
        ed[sl, :] = e
        return total + fold(e, jnp.sum), wanted + fold(hit[sl, :] * d, jnp.sum)

    zero = jnp.zeros((8, r), F32)
    draft_total, wanted = lax.fori_loop(0, n // sb, draft_body, (zero, zero))

    t_recv[0].wait_recv()
    multiply(tl, rows_t, (v, sib), True)
    multiply(tl, rows_t, (left, right), False)
    t_recv[5].wait_recv()
    t_send[9].start()
    t_recv[6].wait_recv()
    t_send[10].start()
    t_recv[7].wait_recv()
    t_recv[8].wait_recv()
    multiply(tl, rows_t, (left_s, right_s), False)
    t_recv[9].wait_recv()
    t_recv[10].wait_recv()
    multiply(tl, rows_t, (opp, opp_s), False)

    teach_max = row_max(tl)

    def teach_body(j, carry):
        total, cross = carry
        sl = pl.ds(pl.multiple_of(j * sb, sb), sb)
        a = tl[sl, :]
        e = jnp.exp(a - teach_max)
        gap = a - dl[sl, :]
        tl[sl, :] = e
        return total + fold(e, jnp.sum), cross + fold(e * gap, jnp.sum)

    teach_total, cross = lax.fori_loop(0, n // sb, teach_body, (zero, zero))

    def down(a):
        return jnp.sum(a, axis=0, keepdims=True)

    for i, row in enumerate(
        (
            teach_max,
            draft_max,
            down(teach_total),
            down(draft_total),
            down(cross),
            down(wanted),
            local_hits,
            jnp.zeros((1, r), F32),
        )
    ):
        stats[v, i : i + 1, :] = row
    st_out = [
        remote(
            stats.at[v], stats.at[v], st_send.at[i - 1], st_recv.at[i - 1],
            {"voc": lax.rem(v + i, 8)},
        )
        for i in range(1, 8)
    ]
    for cp in st_out:
        cp.start()
    for i in range(1, 8):
        p = lax.rem(v + 8 - i, 8)
        remote(
            stats.at[p], stats.at[p], st_send.at[i - 1], st_recv.at[i - 1], {"voc": p}
        ).wait_recv()

    everyone = [stats[i] for i in range(8)]

    def gathered(i):
        return jnp.concatenate([s[i : i + 1, :] for s in everyone], axis=0)

    t_maxes, d_maxes = gathered(0), gathered(1)
    t_max = jnp.max(t_maxes, axis=0, keepdims=True)
    d_max = jnp.max(d_maxes, axis=0, keepdims=True)
    t_scale = jnp.exp(t_maxes - t_max)
    d_scale = jnp.exp(d_maxes - d_max)
    t_total = down(gathered(2) * t_scale)
    d_total = down(gathered(3) * d_scale)
    cross_all = down(gathered(4) * t_scale)
    target_logit = down(gathered(5))
    hits = down(gathered(6))
    slots = lax.broadcasted_iota(jnp.int32, (1, r), 1)
    valid = jnp.where(slots < counts[t], 1.0, 0.0).astype(F32)
    t_lse = t_max + jnp.log(t_total)
    d_lse = d_max + jnp.log(d_total)
    loss[...] = valid * (
        cross_all / t_total - t_lse + d_lse + hits * (d_lse - target_logit)
    )
    d_factor = valid * (1.0 + hits) * jnp.exp(draft_max - d_max) / d_total
    t_factor = valid * jnp.exp(teach_max - t_max) / t_total

    def grad_body(j, carry):
        sl = pl.ds(pl.multiple_of(j * sb, sb), sb)
        g[sl, :] = (d_factor * ed[sl, :] - t_factor * tl[sl, :] - valid * hit[sl, :]).astype(BF16)
        return carry

    lax.fori_loop(0, n // sb, grad_body, 0)

    def back(o, to):
        for b in range(2):
            part[o, b] = jnp.dot(
                head_v[to, b * f : (b + 1) * f, :], g[...], preferred_element_type=F32
            )

    def swap(o):
        return remote(
            part.at[o, 1 - c], sibp.at[o], rs_send.at[o], rs_recv.at[o], {"voc": sib}
        )

    swaps = [swap(o) for o in range(4)]

    def near_sum(o):
        swaps[o].wait_recv()
        return part[o, c] + sibp[o]

    flo, fhi = pl.ds(0, fh), pl.ds(fh, fh)
    out_two_r = remote(two.at[flo], far_l, rs_send.at[4], rs_recv.at[4], {"voc": right})
    out_two_l = remote(two.at[fhi], far_r, rs_send.at[5], rs_recv.at[5], {"voc": left})
    out_r = [
        remote(near.at[0, s], in_l.at[s], rs_send.at[6 + i], rs_recv.at[6 + i], {"voc": right})
        for i, s in enumerate((flo, fhi))
    ]
    out_l = [
        remote(near.at[1, s], in_r.at[s], rs_send.at[8 + i], rs_recv.at[8 + i], {"voc": left})
        for i, s in enumerate((flo, fhi))
    ]

    back(2, xo)
    swaps[2].start()
    back(1, xr)
    swaps[1].start()
    two[...] = near_sum(2).astype(BF16)
    out_two_r.start()
    out_two_l.start()
    back(3, xl)
    swaps[3].start()
    swaps[1].wait_recv()
    near[0, fh:f, :] = (part[1, c, fh:f, :] + sibp[1, fh:f, :]).astype(BF16)
    out_r[1].start()
    swaps[3].wait_recv()
    near[1, 0:fh, :] = (part[3, c, 0:fh, :] + sibp[3, 0:fh, :]).astype(BF16)
    out_l[0].start()
    back(0, x)
    swaps[0].start()
    out_two_r.wait_recv()
    near[0, 0:fh, :] = (
        part[1, c, 0:fh, :] + sibp[1, 0:fh, :] + far_l[...].astype(F32)
    ).astype(BF16)
    out_r[0].start()
    out_two_l.wait_recv()
    near[1, fh:f, :] = (
        part[3, c, fh:f, :] + sibp[3, fh:f, :] + far_r[...].astype(F32)
    ).astype(BF16)
    out_l[1].start()
    mine = near_sum(0)
    for cp in out_r + out_l:
        cp.wait_recv()
    total = mine + in_l[...].astype(F32) + in_r[...].astype(F32)
    grad[...] = (loss_scale * total).T.astype(BF16)

    for cp in d_send + t_send + repack + st_out + swaps + [out_two_r, out_two_l] + out_r + out_l:
        cp.wait_send()


def per_device(n_tok, teacher_rows, drafter_rows, head, fr_ids, targets, dest_index, counts):
    r, f = teacher_rows.shape
    d, n = head.shape
    dma = pltpu.SemaphoreType.DMA
    any_spec = pl.BlockSpec(memory_space=pl.ANY)
    vmem = pl.BlockSpec(memory_space=pltpu.VMEM)
    row_loss, grad = pl.pallas_call(
        functools.partial(kernel, n_tok),
        out_shape=(
            jax.ShapeDtypeStruct((1, r), F32),
            jax.ShapeDtypeStruct((r, f), BF16),
        ),
        in_specs=[any_spec, any_spec, any_spec, vmem, vmem, vmem,
                  pl.BlockSpec(memory_space=pltpu.SMEM)],
        out_specs=(vmem, vmem),
        scratch_shapes=[
            pltpu.VMEM((4, 2 * f, n), BF16),
            pltpu.VMEM((8, n, f), BF16),
            pltpu.VMEM((8, r, f), BF16),
            pltpu.VMEM((8, r, f), BF16),
            pltpu.VMEM((r, f), BF16),
            pltpu.VMEM((4, r // 4 + 16, f), BF16),
            pltpu.VMEM((4, r // 4 + 16, f), BF16),
            pltpu.VMEM((n, r), F32),
            pltpu.VMEM((n, r), F32),
            pltpu.VMEM((n, r), F32),
            pltpu.VMEM((n, r), F32),
            pltpu.VMEM((n, r), BF16),
            pltpu.VMEM((4, 2, f, r), F32),
            pltpu.VMEM((4, f, r), F32),
            pltpu.VMEM((f, r), BF16),
            pltpu.VMEM((f // 2, r), BF16),
            pltpu.VMEM((f // 2, r), BF16),
            pltpu.VMEM((2, f, r), BF16),
            pltpu.VMEM((f, r), BF16),
            pltpu.VMEM((f, r), BF16),
            pltpu.VMEM((8, 8, r), F32),
            dma((6,)),
            dma((2, 11)),
            dma((2, 11)),
            dma((4,)),
            dma((4,)),
            dma((7,)),
            dma((7,)),
            dma((10,)),
            dma((10,)),
        ],
        compiler_params=pltpu.CompilerParams(
            collective_id=0, has_side_effects=True, vmem_limit_bytes=56 * 1024 * 1024
        ),
    )(
        teacher_rows,
        drafter_rows,
        head,
        fr_ids.reshape(1, n),
        targets.reshape(1, r),
        dest_index.reshape(1, r),
        counts,
    )
    return row_loss.reshape(r), grad


def solution(mesh):
    return jax.shard_map(
        functools.partial(per_device, mesh.shape["tok"]),
        mesh=mesh,
        in_specs=(
            P("tok", "voc"),
            P("tok", "voc"),
            P(None, "voc"),
            P("voc"),
            P("tok"),
            P("tok"),
            P(),
        ),
        out_specs=(P("tok"), P("tok", "voc")),
        check_vma=False,
    )
```

time: 240 us -> 48.2 us (0.20)
  waiting for transfers between devices: 126 us -> 0 us
  blocking collectives: 64.2 us -> 0 us
  Pallas kernels: 0 us -> 44.4 us
  matrix products: 25.9 us -> 0 us
  between operations: 13.8 us -> 0.64 us
  other arithmetic: 7.13 us -> 0 us
    all_gather x3 -> x0, waiting for transfers between devices: 92.3 us -> none  [the longest x1 46.4 us: per_device(): rows_piece = lax.all_gather(teacher_rows, 'tok', axis=0, tiled=True)]
    pallas_call x0 -> x1, Pallas kernels: none -> 44.4 us  [per_device(): pl.pallas_call(functools.partial(kernel, n_tok), out_shape=(jax.ShapeDtyp...]
    all_gather x1 -> x0, blocking collectives: 37.7 us -> none  [per_device(): code_piece = lax.all_gather(code, 'tok', axis=0, tiled=True)]
    reduce_scatter x1 -> x0, waiting for transfers between devices: 32.6 us -> none  [per_device(): lax.psum_scatter(lax.dot_general(head, grad_logit, (((1,), (1,)), ((), ()...]
    dot_general x4 -> x0, matrix products: 25.9 us -> none  [the longest x1 8.28 us: per_device(): lax.dot_general(head, grad_logit, (((1,), (1,)), ((), ())), preferred_ele...]
    psum x1 -> x0, blocking collectives: 14.5 us -> none  [per_device(): lax.psum((jnp.sum(teach_exp, axis=1), jnp.sum(draft_exp, axis=1), jnp.sum...]
    pmax x1 -> x0, blocking collectives: 12 us -> none  [per_device(): lax.pmax((jnp.max(teach_logit, axis=1), jnp.max(draft_logit, axis=1)), 'v...]
    reduce_sum x1 -> x0, other arithmetic: 3.04 us -> none  [per_device(): jnp.sum(teach_exp * (teach_logit - draft_logit), axis=1)]
  transfers between devices with their start and end apart: 4 -> 0, of which waited for: 4 -> 0; matrix products, arithmetic and copies ran while one was open for 5% -> 0% of each run, Pallas kernels for 0% -> 0%
where the time goes in v1:
time: 48.2 us; the launch traced here: 47.9 us
  Pallas kernels  44.4 us (92%)
  local copies, waits for them, and re-layouts  2.8 us (6%)
  between operations  0.64 us (1%)
    pallas_call x1, Pallas kernels, per_device(): pl.pallas_call(functools.partial(kernel, n_tok), out_shape=(jax.ShapeDtyp...  44.4 us
    unnamed x2, local copies, waits for them, and re-layouts  2.8 us

profile of v1, /device:TPU:1, one launch (start us, length us, event | category | flops | bytes accessed | tf_op | source)
XLA Modules:
  0.0 47.9 jit_solution(8846866174331456168)
XLA Ops:
  0.6 44.4 %shard_map.86 = (f32[1,256]{1,0:T(1,128)}, bf16[256,256]{1,0:T(8,128)(2,1)}) custom-call(bf16[256,256]{1,0:T(8,128)(2,1)} %teach.1, bf16[256,256]{1,0:T(8,128)(2,1)} %draft.1, bf16[2048,2048]{1,0:T(8,128)(2,1)} %head.1, s32[1,2048]{1,0:T(1,128)} %bitcast.4, s32[1,256]{1,0:T(1,128)} %bitcast.5, s32[1,256]{1,0:T(1,128)} %bitcast.6, s32[32]{0:T(128)} %counts.1), custom_call_target="tpu_custom_call" | custom-call | tf_op jit(solution)/shard_map/pallas_call | solution.py:461
  45.1 1.2 %copy.11 = f32[256]{0:T(256)} copy(f32[256]{0:T(256)} %bitcast.7) | data formatting | bytes 2048
  46.3 1.6 %copy.12 = bf16[256,256]{1,0:T(8,128)(2,1)} copy(bf16[256,256]{1,0:T(8,128)(2,1)} %get-tuple-element.9) | data formatting | bytes 262144

commit v2 on v1

v2 whole, which is shorter than its diff:
```python
import functools

import jax
import jax.numpy as jnp
from jax import lax
from jax.experimental import pallas as pl
from jax.experimental.pallas import tpu as pltpu
from jax.sharding import PartitionSpec as P

loss_scale = 16.0
MESH = pl.DeviceIdType.MESH
NT = (((1,), (1,)), ((), ()))
F32 = jnp.float32
BF16 = jnp.bfloat16


def kernel(
    n_tok,
    teach,
    draft,
    head,
    fr_hbm,
    targ_hbm,
    dest_hbm,
    counts_hbm,
    loss,
    grad,
    fr,
    targ,
    dest,
    counts,
    head_v,
    head_t,
    rows_d,
    rows_t,
    teach_v,
    pack,
    got,
    tl,
    dl,
    ed,
    hit,
    g,
    part,
    sibp,
    two,
    far,
    near,
    inn,
    stats,
    load_sem,
    ag_send,
    ag_recv,
    pk_sem,
    st_sem,
    rs_send,
    rs_recv,
):
    n, r = hit.shape
    f = teach.shape[1]
    quarter = r // 4
    half = r // 2
    fh = f // 2
    shifts = (0, 1, n_tok // 2, n_tok // 2 + 1)
    t = lax.axis_index("tok")
    v = lax.axis_index("voc")
    x = lax.div(v, 2)
    c = lax.rem(v, 2)
    xr = lax.rem(x + 1, 4)
    xl = lax.rem(x + 3, 4)
    xo = lax.rem(x + 2, 4)
    sib = x * 2 + 1 - c
    right = xr * 2 + c
    left = xl * 2 + c
    opp = xo * 2 + c
    right_s = xr * 2 + 1 - c
    left_s = xl * 2 + 1 - c
    opp_s = xo * 2 + 1 - c

    barrier = pltpu.get_barrier_semaphore()
    for k in shifts[1:]:
        pl.semaphore_signal(
            barrier, inc=1, device_id={"tok": lax.rem(t + n_tok - k, n_tok)}, device_id_type=MESH
        )
    for p in (sib, right, left):
        pl.semaphore_signal(barrier, inc=1, device_id={"voc": p}, device_id_type=MESH)

    load_d = pltpu.make_async_copy(draft, rows_d.at[v], load_sem.at[0])
    load_t = pltpu.make_async_copy(teach, teach_v, load_sem.at[1])
    load_h = [
        pltpu.make_async_copy(
            head.at[pl.ds(i * 2 * f, 2 * f)], head_v.at[i], load_sem.at[2 + i]
        )
        for i in range(4)
    ]
    load_s = [
        pltpu.make_async_copy(a, b, load_sem.at[6 + i])
        for i, (a, b) in enumerate(
            ((dest_hbm, dest), (targ_hbm, targ), (fr_hbm, fr), (counts_hbm, counts))
        )
    ]
    load_s[0].start()
    load_t.start()
    load_d.start()
    for cp in load_s[1:]:
        cp.start()

    def remote(src, dst, ssem, rsem, to):
        return pltpu.make_async_remote_copy(
            src_ref=src, dst_ref=dst, send_sem=ssem, recv_sem=rsem,
            device_id=to, device_id_type=MESH,
        )

    lo, hi = pl.ds(0, half), pl.ds(half, half)

    def gather(q, rows):
        def piece(i, p, to, h=None):
            ref = rows.at[p] if h is None else rows.at[p, h]
            return remote(ref, ref, ag_send.at[q], ag_recv.at[q, i], {"voc": to})

        send = [
            piece(0, v, sib),
            piece(1, v, right, lo),
            piece(2, v, right, hi),
            piece(1, v, left, hi),
            piece(2, v, left, lo),
            piece(3, left, right, lo),
            piece(3, right, left, hi),
            piece(4, left, sib),
            piece(4, right, sib),
            piece(5, opp, sib, lo),
            piece(5, opp, sib, hi),
        ]
        one = rows.at[v]
        pair = rows.at[pl.ds(0, 2)]
        recv = [
            remote(ref, ref, ag_send.at[q], ag_recv.at[q, i], {"voc": sib})
            for i, ref in enumerate((one, one, one, one, pair, one))
        ]
        seven = rows.at[pl.ds(0, 7)]
        return send, recv, remote(seven, seven, ag_send.at[q], ag_recv.at[q, 0], {"voc": sib})

    d_send, d_recv, d_all = gather(0, rows_d)
    t_send, t_recv, t_all = gather(1, rows_t)

    load_s[0].wait()
    load_t.wait()
    for cp in load_h:
        cp.start()
    dest_row = dest[...]
    place = lax.rem(dest_row + r, quarter)
    spot = lax.broadcasted_iota(jnp.int32, (quarter, r), 0)
    picks = []
    sizes = []
    for k in shifts:
        rel = dest_row - lax.rem(t + k, n_tok) * r
        inside = (rel >= 0) & (rel < r)
        picks.append(jnp.where(jnp.where(inside, place, -1) == spot, 1.0, 0.0).astype(F32))
        sizes.append(jnp.sum(jnp.where(inside, 1.0, 0.0).astype(F32), axis=1, keepdims=True))
    picked = jnp.dot(
        jnp.concatenate(picks, axis=0).astype(BF16), teach_v[...], preferred_element_type=F32
    ).astype(BF16)
    for i in range(4):
        pack[i, 0:quarter, :] = picked[i * quarter : (i + 1) * quarter, :]
        pack[i, quarter : quarter + 16, :] = jnp.broadcast_to(sizes[i], (16, f)).astype(BF16)
    repack = [
        remote(
            pack.at[i], got.at[i], pk_sem.at[0], pk_sem.at[1],
            {"tok": lax.rem(t + shifts[i], n_tok)},
        )
        for i in range(1, 4)
    ]
    pl.semaphore_wait(barrier, 6)
    for cp in repack:
        cp.start()
    load_d.wait()
    for i in (1, 3, 2, 4, 0):
        d_send[i].start()

    for cp in load_s[1:]:
        cp.wait()
    targets = targ[...].astype(F32)
    hits_sum = jnp.zeros((8, r), F32)
    for j in range(n // 128):
        ids = fr[0:1, j * 128 : (j + 1) * 128].astype(F32)
        ids = jnp.broadcast_to(ids, (128, 128)).T
        ids = jnp.concatenate([ids] * (r // 128), axis=1) if r >= 128 else ids[:, :r]
        h = jnp.where(ids == targets, 1.0, 0.0).astype(F32)
        hit[j * 128 : (j + 1) * 128, :] = h
        hits_sum = hits_sum + jnp.sum(h.reshape(16, 8, r), axis=0)
    local_hits = jnp.sum(hits_sum, axis=0, keepdims=True)

    def turn(i):
        load_h[i].wait()
        for b in range(2):
            for j in range(n // 256):
                head_t[2 * i + b, j * 256 : (j + 1) * 256, :] = head_v[
                    i, b * f : (b + 1) * f, j * 256 : (j + 1) * 256
                ].T

    all_packs = remote(
        pack.at[pl.ds(1, 3)], got.at[pl.ds(1, 3)], pk_sem.at[0], pk_sem.at[1], {"voc": sib}
    )
    turn(0)
    turn(1)
    d_recv[1].wait_recv()
    d_send[5].start()
    d_send[6].start()
    all_packs.wait_recv()
    one = [got[i, quarter : quarter + 1, :].astype(F32) for i in range(1, 4)]
    start = [jnp.full((1, f), float(quarter), F32)]
    for i in range(2):
        start.append(start[-1] + one[i])
    rows_t[v, 0:quarter, :] = pack[0, 0:quarter, :]
    for q in range(1, 4):
        slot = lax.broadcasted_iota(jnp.int32, (quarter, f), 0).astype(F32) + float(q * quarter)
        total = jnp.zeros((quarter, f), F32)
        for i in range(3):
            mine = (slot >= start[i]) & (slot < start[i] + one[i])
            total = total + jnp.where(mine, got[i + 1, 0:quarter, :].astype(F32), 0.0)
        rows_t[v, q * quarter : (q + 1) * quarter, :] = total.astype(BF16)
    for i in (1, 3, 2, 4, 0):
        t_send[i].start()

    d_recv[2].wait_recv()
    d_send[7].start()
    d_send[8].start()
    turn(2)
    turn(3)
    d_recv[3].wait_recv()
    d_send[9].start()
    d_send[10].start()

    def multiply(acc, rows, ks, first):
        @pl.when(v >= 0)
        def _():
            a = jnp.concatenate([head_t[k] for k in ks], axis=1)
            b = jnp.concatenate([rows[k] for k in ks], axis=1)
            s = lax.dot_general(a, b, NT, preferred_element_type=F32)
            acc[...] = s if first else acc[...] + s

    sb = min(n, 256)

    def fold(a, op):
        return op(a.reshape(sb // 8, 8, r), axis=0)

    def row_max(acc):
        def body(j, m):
            sl = pl.ds(pl.multiple_of(j * sb, sb), sb)
            return jnp.maximum(m, fold(acc[sl, :], jnp.max))

        m = lax.fori_loop(0, n // sb, body, jnp.full((8, r), -jnp.inf, F32))
        return jnp.max(m, axis=0, keepdims=True)

    d_recv[0].wait_recv()
    multiply(dl, rows_d, (v, sib, left, right), True)
    t_recv[1].wait_recv()
    t_send[5].start()
    t_send[6].start()
    d_recv[4].wait_recv()
    d_recv[5].wait_recv()
    multiply(dl, rows_d, (left_s, right_s, opp, opp_s), False)
    t_recv[2].wait_recv()
    t_send[7].start()
    t_send[8].start()
    t_recv[0].wait_recv()
    multiply(tl, rows_t, (v, sib, left, right), True)
    t_recv[3].wait_recv()
    t_send[9].start()
    t_send[10].start()
    draft_max = row_max(dl)

    def draft_body(j, carry):
        total, wanted = carry
        sl = pl.ds(pl.multiple_of(j * sb, sb), sb)
        d = dl[sl, :]
        e = jnp.exp(d - draft_max)
        ed[sl, :] = e
        return total + fold(e, jnp.sum), wanted + fold(hit[sl, :] * d, jnp.sum)

    zero = jnp.zeros((8, r), F32)
    draft_total, wanted = lax.fori_loop(0, n // sb, draft_body, (zero, zero))

    t_recv[4].wait_recv()
    multiply(tl, rows_t, (left_s, right_s), False)
    t_recv[5].wait_recv()
    multiply(tl, rows_t, (opp, opp_s), False)

    teach_max = row_max(tl)

    def teach_body(j, carry):
        total, cross = carry
        sl = pl.ds(pl.multiple_of(j * sb, sb), sb)
        a = tl[sl, :]
        e = jnp.exp(a - teach_max)
        gap = a - dl[sl, :]
        tl[sl, :] = e
        return total + fold(e, jnp.sum), cross + fold(e * gap, jnp.sum)

    teach_total, cross = lax.fori_loop(0, n // sb, teach_body, (zero, zero))

    def down(a):
        return jnp.sum(a, axis=0, keepdims=True)

    for i, row in enumerate(
        (
            teach_max,
            draft_max,
            down(teach_total),
            down(draft_total),
            down(cross),
            down(wanted),
            local_hits,
            jnp.zeros((1, r), F32),
        )
    ):
        stats[v, i : i + 1, :] = row
    st_out = [
        remote(stats.at[v], stats.at[v], st_sem.at[0], st_sem.at[1], {"voc": p})
        for p in (opp, opp_s, right, right_s, left, left_s, sib)
    ]
    for cp in st_out:
        cp.start()
    seven = stats.at[pl.ds(0, 7)]
    all_stats = remote(seven, seven, st_sem.at[0], st_sem.at[1], {"voc": sib})
    all_stats.wait_recv()

    everyone = [stats[i] for i in range(8)]

    def gathered(i):
        return jnp.concatenate([s[i : i + 1, :] for s in everyone], axis=0)

    t_maxes, d_maxes = gathered(0), gathered(1)
    t_max = jnp.max(t_maxes, axis=0, keepdims=True)
    d_max = jnp.max(d_maxes, axis=0, keepdims=True)
    t_scale = jnp.exp(t_maxes - t_max)
    d_scale = jnp.exp(d_maxes - d_max)
    t_total = down(gathered(2) * t_scale)
    d_total = down(gathered(3) * d_scale)
    cross_all = down(gathered(4) * t_scale)
    target_logit = down(gathered(5))
    hits = down(gathered(6))
    slots = lax.broadcasted_iota(jnp.int32, (1, r), 1)
    valid = jnp.where(slots < counts[t], 1.0, 0.0).astype(F32)
    t_lse = t_max + jnp.log(t_total)
    d_lse = d_max + jnp.log(d_total)
    loss[...] = valid * (
        cross_all / t_total - t_lse + d_lse + hits * (d_lse - target_logit)
    )
    d_factor = valid * (1.0 + hits) * jnp.exp(draft_max - d_max) / d_total
    t_factor = valid * jnp.exp(teach_max - t_max) / t_total

    def grad_body(j, carry):
        sl = pl.ds(pl.multiple_of(j * sb, sb), sb)
        g[sl, :] = (d_factor * ed[sl, :] - t_factor * tl[sl, :] - valid * hit[sl, :]).astype(BF16)
        return carry

    lax.fori_loop(0, n // sb, grad_body, 0)

    def back(o, to, which):
        @pl.when(v >= 0)
        def _():
            for b in which:
                rows = pl.ds(b * f, f)
                if not isinstance(b, int):
                    rows = pl.ds(pl.multiple_of(b * f, f), f)
                part[o, b] = jnp.dot(head_v[to, rows, :], g[...], preferred_element_type=F32)

    swaps = [
        remote(part.at[o, 1 - c], sibp.at[o], rs_send.at[0], rs_recv.at[o], {"voc": sib})
        for o in range(4)
    ]

    flo, fhi = pl.ds(0, fh), pl.ds(fh, fh)
    out_two_r = remote(two.at[flo], far.at[flo], rs_send.at[1], rs_recv.at[4], {"voc": right})
    out_two_l = remote(two.at[fhi], far.at[fhi], rs_send.at[1], rs_recv.at[5], {"voc": left})

    def out_near(i, h, to):
        return remote(near.at[i, h], inn.at[i, h], rs_send.at[2], rs_recv.at[6], {"voc": to})

    back(2, xo, (1 - c,))
    swaps[2].start()
    back(2, xo, (c,))
    back(1, xr, (0, 1))
    swaps[1].start()
    swaps[2].wait_recv()
    two[...] = (part[2, c] + sibp[2]).astype(BF16)
    out_two_r.start()
    out_two_l.start()
    back(3, xl, (0, 1))
    swaps[3].start()
    swaps[1].wait_recv()
    near[0, fh:f, :] = (part[1, c, fh:f, :] + sibp[1, fh:f, :]).astype(BF16)
    out_near(0, fhi, right).start()
    back(0, x, (0, 1))
    swaps[0].start()
    swaps[3].wait_recv()
    near[1, 0:fh, :] = (part[3, c, 0:fh, :] + sibp[3, 0:fh, :]).astype(BF16)
    out_near(1, flo, left).start()
    out_two_r.wait_recv()
    near[0, 0:fh, :] = (
        part[1, c, 0:fh, :] + sibp[1, 0:fh, :] + far[0:fh, :].astype(F32)
    ).astype(BF16)
    out_near(0, flo, right).start()
    out_two_l.wait_recv()
    near[1, fh:f, :] = (
        part[3, c, fh:f, :] + sibp[3, fh:f, :] + far[fh:f, :].astype(F32)
    ).astype(BF16)
    out_near(1, fhi, left).start()
    swaps[0].wait_recv()
    mine = part[0, c] + sibp[0]
    both = remote(near, inn, rs_send.at[2], rs_recv.at[6], {"voc": sib})
    both.wait_recv()
    total = mine + inn[0].astype(F32) + inn[1].astype(F32)
    grad[...] = (loss_scale * total).T.astype(BF16)

    all_swaps = remote(sibp, sibp, rs_send.at[0], rs_recv.at[0], {"voc": sib})
    all_two = remote(two, far, rs_send.at[1], rs_recv.at[4], {"voc": sib})
    for cp in (d_all, t_all, all_packs, all_stats, all_swaps, all_two, both):
        cp.wait_send()


def per_device(n_tok, teacher_rows, drafter_rows, head, fr_ids, targets, dest_index, counts):
    r, f = teacher_rows.shape
    d, n = head.shape
    dma = pltpu.SemaphoreType.DMA
    any_spec = pl.BlockSpec(memory_space=pl.ANY)
    vmem = pl.BlockSpec(memory_space=pltpu.VMEM)
    row_loss, grad = pl.pallas_call(
        functools.partial(kernel, n_tok),
        out_shape=(
            pltpu.VMEM((1, r), F32),
            pltpu.VMEM((r, f), BF16),
        ),
        in_specs=[any_spec] * 7,
        out_specs=(vmem, vmem),
        scratch_shapes=[
            pltpu.VMEM((1, n), jnp.int32),
            pltpu.VMEM((1, r), jnp.int32),
            pltpu.VMEM((1, r), jnp.int32),
            pltpu.SMEM((n_tok,), jnp.int32),
            pltpu.VMEM((4, 2 * f, n), BF16),
            pltpu.VMEM((8, n, f), BF16),
            pltpu.VMEM((8, r, f), BF16),
            pltpu.VMEM((8, r, f), BF16),
            pltpu.VMEM((r, f), BF16),
            pltpu.VMEM((4, r // 4 + 16, f), BF16),
            pltpu.VMEM((4, r // 4 + 16, f), BF16),
            pltpu.VMEM((n, r), F32),
            pltpu.VMEM((n, r), F32),
            pltpu.VMEM((n, r), F32),
            pltpu.VMEM((n, r), F32),
            pltpu.VMEM((n, r), BF16),
            pltpu.VMEM((4, 2, f, r), F32),
            pltpu.VMEM((4, f, r), F32),
            pltpu.VMEM((f, r), BF16),
            pltpu.VMEM((f, r), BF16),
            pltpu.VMEM((2, f, r), BF16),
            pltpu.VMEM((2, f, r), BF16),
            pltpu.VMEM((8, 8, r), F32),
            dma((10,)),
            dma((2,)),
            dma((2, 6)),
            dma((2,)),
            dma((2,)),
            dma((3,)),
            dma((7,)),
        ],
        compiler_params=pltpu.CompilerParams(
            collective_id=0, has_side_effects=True, vmem_limit_bytes=56 * 1024 * 1024
        ),
    )(
        teacher_rows,
        drafter_rows,
        head,
        fr_ids.reshape(1, n),
        targets.reshape(1, r),
        dest_index.reshape(1, r),
        counts,
    )
    return row_loss.reshape(r), grad


def solution(mesh):
    return jax.shard_map(
        functools.partial(per_device, mesh.shape["tok"]),
        mesh=mesh,
        in_specs=(
            P("tok", "voc"),
            P("tok", "voc"),
            P(None, "voc"),
            P("voc"),
            P("tok"),
            P("tok"),
            P(),
        ),
        out_specs=(P("tok"), P("tok", "voc")),
        check_vma=False,
    )
```

time: 48.2 us -> 39.4 us (0.82)
  Pallas kernels: 44.4 us -> 37.3 us
  local copies, waits for them, and re-layouts: 2.8 us -> 1.22 us
    pallas_call x1, Pallas kernels: 44.4 us -> 37.3 us  [per_device(): pl.pallas_call(functools.partial(kernel, n_tok), out_shape=(pltpu.VMEM((1...]
    unnamed x2, local copies, waits for them, and re-layouts: 2.8 us -> 1.22 us
where the time goes in v2:
time: 39.4 us; the launch traced here: 39.2 us
  Pallas kernels  37.3 us (95%)
  local copies, waits for them, and re-layouts  1.22 us (3%)
  between operations  0.64 us (2%)
    pallas_call x1, Pallas kernels, per_device(): pl.pallas_call(functools.partial(kernel, n_tok), out_shape=(pltpu.VMEM((1...  37.3 us
    unnamed x2, local copies, waits for them, and re-layouts  1.22 us

profile of v2, /device:TPU:1, one launch (start us, length us, event | category | flops | bytes accessed | tf_op | source)
XLA Modules:
  0.0 39.2 jit_solution(7383307006673354422)
XLA Ops:
  0.6 37.3 %shard_map.86 = (f32[1,256]{1,0:T(1,128)S(1)}, bf16[256,256]{1,0:T(8,128)(2,1)S(1)}) custom-call(bf16[256,256]{1,0:T(8,128)(2,1)} %teach.1, bf16[256,256]{1,0:T(8,128)(2,1)} %draft.1, bf16[2048,2048]{1,0:T(8,128)(2,1)} %head.1, s32[1,2048]{1,0:T(1,128)} %bitcast.5, s32[1,256]{1,0:T(1,128)} %bitcast.6, s32[1,256]{1,0:T(1,128)} %bitcast.7, s32[32]{0:T(128)} %counts_hbm.1), custom_call_target="tpu_custom_call" | custom-call | tf_op jit(solution)/shard_map/pallas_call | solution.py:429
  38.0 0.6 %copy.11 = f32[256]{0:T(256)} copy(f32[256]{0:T(256)S(1)} %bitcast.4) | data formatting | bytes 2048
  38.5 0.7 %copy.12 = bf16[256,256]{1,0:T(8,128)(2,1)} copy(bf16[256,256]{1,0:T(8,128)(2,1)S(1)} %get-tuple-element.7) | data formatting | bytes 262144

commit v3 on v2

--- a/solution.py
+++ b/solution.py
@@ -43,14 +43,18 @@
     g,
     part,
     sibp,
+    far_part,
+    swap_two,
     two,
     far,
     near,
     inn,
     stats,
+    top,
     load_sem,
     ag_send,
     ag_recv,
+    ea_recv,
     pk_sem,
     st_sem,
     rs_send,
@@ -59,7 +63,6 @@
     n, r = hit.shape
     f = teach.shape[1]
     quarter = r // 4
-    half = r // 2
     fh = f // 2
     shifts = (0, 1, n_tok // 2, n_tok // 2 + 1)
     t = lax.axis_index("tok")
@@ -102,7 +105,7 @@
     load_s[0].start()
     load_t.start()
     load_d.start()
-    for cp in load_s[1:]:
+    for cp in load_s[1:] + load_h:
         cp.start()
 
     def remote(src, dst, ssem, rsem, to):
@@ -111,11 +114,13 @@
             device_id=to, device_id_type=MESH,
         )
 
-    lo, hi = pl.ds(0, half), pl.ds(half, half)
-
-    def gather(q, rows):
+    def gather(q, rows, skip):
+        h = (r - skip) // 2
+        lo, hi = pl.ds(skip, h), pl.ds(skip + h, h)
+        every = pl.ds(skip, 2 * h)
+
         def piece(i, p, to, h=None):
-            ref = rows.at[p] if h is None else rows.at[p, h]
+            ref = rows.at[p, every] if h is None else rows.at[p, h]
             return remote(ref, ref, ag_send.at[q], ag_recv.at[q, i], {"voc": to})
 
         send = [
@@ -131,22 +136,34 @@
             piece(5, opp, sib, lo),
             piece(5, opp, sib, hi),
         ]
-        one = rows.at[v]
-        pair = rows.at[pl.ds(0, 2)]
+        one = rows.at[v, every]
+        pair = rows.at[pl.ds(0, 2), every]
         recv = [
             remote(ref, ref, ag_send.at[q], ag_recv.at[q, i], {"voc": sib})
             for i, ref in enumerate((one, one, one, one, pair, one))
         ]
-        seven = rows.at[pl.ds(0, 7)]
+        seven = rows.at[pl.ds(0, 7), every]
         return send, recv, remote(seven, seven, ag_send.at[q], ag_recv.at[q, 0], {"voc": sib})
 
-    d_send, d_recv, d_all = gather(0, rows_d)
-    t_send, t_recv, t_all = gather(1, rows_t)
+    d_send, d_recv, d_all = gather(0, rows_d, 0)
+    t_send, t_recv, t_all = gather(1, rows_t, quarter)
+
+    kept = pl.ds(0, quarter)
+
+    def early(p, to, i):
+        ref = rows_t.at[p, kept]
+        return remote(ref, ref, ag_send.at[2], ea_recv.at[i], {"voc": to})
+
+    def early_wait(count, i):
+        ref = rows_t.at[pl.ds(0, count), kept]
+        return remote(ref, ref, ag_send.at[2], ea_recv.at[i], {"voc": sib})
+
+    early_near = [early(v, right, 0), early(v, left, 0), early(v, sib, 1)]
+    early_far = early(v, opp, 0)
+    early_pass = [early(p, sib, 1) for p in (left, right, opp)]
 
     load_s[0].wait()
     load_t.wait()
-    for cp in load_h:
-        cp.start()
     dest_row = dest[...]
     place = lax.rem(dest_row + r, quarter)
     spot = lax.broadcasted_iota(jnp.int32, (quarter, r), 0)
@@ -170,11 +187,12 @@
         )
         for i in range(1, 4)
     ]
+    rows_t[v, 0:quarter, :] = pack[0, 0:quarter, :]
     pl.semaphore_wait(barrier, 6)
     for cp in repack:
         cp.start()
     load_d.wait()
-    for i in (1, 3, 2, 4, 0):
+    for i in (1, 3, 0):
         d_send[i].start()
 
     for cp in load_s[1:]:
@@ -202,16 +220,25 @@
         pack.at[pl.ds(1, 3)], got.at[pl.ds(1, 3)], pk_sem.at[0], pk_sem.at[1], {"voc": sib}
     )
     turn(0)
+    d_send[2].start()
+    d_send[4].start()
     turn(1)
+    turn(2)
+    for cp in early_near:
+        cp.start()
     d_recv[1].wait_recv()
     d_send[5].start()
     d_send[6].start()
+    early_far.start()
+    turn(3)
+    d_recv[2].wait_recv()
+    d_send[7].start()
+    d_send[8].start()
     all_packs.wait_recv()
     one = [got[i, quarter : quarter + 1, :].astype(F32) for i in range(1, 4)]
     start = [jnp.full((1, f), float(quarter), F32)]
     for i in range(2):
         start.append(start[-1] + one[i])
-    rows_t[v, 0:quarter, :] = pack[0, 0:quarter, :]
     for q in range(1, 4):
         slot = lax.broadcasted_iota(jnp.int32, (quarter, f), 0).astype(F32) + float(q * quarter)
         total = jnp.zeros((quarter, f), F32)
@@ -219,56 +246,49 @@
             mine = (slot >= start[i]) & (slot < start[i] + one[i])
             total = total + jnp.where(mine, got[i + 1, 0:quarter, :].astype(F32), 0.0)
         rows_t[v, q * quarter : (q + 1) * quarter, :] = total.astype(BF16)
-    for i in (1, 3, 2, 4, 0):
+    for i in (1, 3, 0):
         t_send[i].start()
-
-    d_recv[2].wait_recv()
-    d_send[7].start()
-    d_send[8].start()
-    turn(2)
-    turn(3)
-    d_recv[3].wait_recv()
-    d_send[9].start()
-    d_send[10].start()
-
-    def multiply(acc, rows, ks, first):
+    def multiply(acc, rows, ks, first, last=False):
         @pl.when(v >= 0)
         def _():
             a = jnp.concatenate([head_t[k] for k in ks], axis=1)
             b = jnp.concatenate([rows[k] for k in ks], axis=1)
             s = lax.dot_general(a, b, NT, preferred_element_type=F32)
-            acc[...] = s if first else acc[...] + s
+            if not first:
+                s = acc[...] + s
+            acc[...] = s
+            if last:
+                top[...] = jnp.max(s.reshape(n // 8, 8, r), axis=0)
 
     sb = min(n, 256)
 
     def fold(a, op):
         return op(a.reshape(sb // 8, 8, r), axis=0)
 
-    def row_max(acc):
-        def body(j, m):
-            sl = pl.ds(pl.multiple_of(j * sb, sb), sb)
-            return jnp.maximum(m, fold(acc[sl, :], jnp.max))
-
-        m = lax.fori_loop(0, n // sb, body, jnp.full((8, r), -jnp.inf, F32))
-        return jnp.max(m, axis=0, keepdims=True)
-
     d_recv[0].wait_recv()
     multiply(dl, rows_d, (v, sib, left, right), True)
+    t_send[2].start()
+    t_send[4].start()
+
+    @pl.when(v >= 0)
+    def _():
+        ones = hit[...].astype(BF16)
+        far_part[2] = jnp.dot(head_v[xo], ones, preferred_element_type=F32)
+
+    d_recv[3].wait_recv()
+    d_send[9].start()
+    d_send[10].start()
+    early_wait(3, 0).wait_recv()
+    for cp in early_pass:
+        cp.start()
+    d_recv[4].wait_recv()
+    multiply(dl, rows_d, (left_s, right_s), False)
     t_recv[1].wait_recv()
     t_send[5].start()
     t_send[6].start()
-    d_recv[4].wait_recv()
     d_recv[5].wait_recv()
-    multiply(dl, rows_d, (left_s, right_s, opp, opp_s), False)
-    t_recv[2].wait_recv()
-    t_send[7].start()
-    t_send[8].start()
-    t_recv[0].wait_recv()
-    multiply(tl, rows_t, (v, sib, left, right), True)
-    t_recv[3].wait_recv()
-    t_send[9].start()
-    t_send[10].start()
-    draft_max = row_max(dl)
+    multiply(dl, rows_d, (opp, opp_s), False, True)
+    draft_max = jnp.max(top[...], axis=0, keepdims=True)
 
     def draft_body(j, carry):
         total, wanted = carry
@@ -281,12 +301,21 @@
     zero = jnp.zeros((8, r), F32)
     draft_total, wanted = lax.fori_loop(0, n // sb, draft_body, (zero, zero))
 
+    t_recv[2].wait_recv()
+    t_send[7].start()
+    t_send[8].start()
+    t_recv[0].wait_recv()
+    early_wait(4, 1).wait_recv()
+    multiply(tl, rows_t, (v, sib, left, right), True)
+    t_recv[3].wait_recv()
+    t_send[9].start()
+    t_send[10].start()
     t_recv[4].wait_recv()
     multiply(tl, rows_t, (left_s, right_s), False)
     t_recv[5].wait_recv()
-    multiply(tl, rows_t, (opp, opp_s), False)
-
-    teach_max = row_max(tl)
+    multiply(tl, rows_t, (opp, opp_s), False, True)
+
+    teach_max = jnp.max(top[...], axis=0, keepdims=True)
 
     def teach_body(j, carry):
         total, cross = carry
@@ -323,6 +352,19 @@
         cp.start()
     seven = stats.at[pl.ds(0, 7)]
     all_stats = remote(seven, seven, st_sem.at[0], st_sem.at[1], {"voc": sib})
+
+    def unscaled(i, ref):
+        @pl.when(v >= 0)
+        def _():
+            e = ref[...]
+            top_bits = e.astype(BF16)
+            rest = (e - top_bits.astype(F32)).astype(BF16)
+            far_part[i] = jnp.dot(head_v[xo], top_bits, preferred_element_type=F32) + jnp.dot(
+                head_v[xo], rest, preferred_element_type=F32
+            )
+
+    unscaled(0, ed)
+    unscaled(1, tl)
     all_stats.wait_recv()
 
     everyone = [stats[i] for i in range(8)]
@@ -350,43 +392,52 @@
     d_factor = valid * (1.0 + hits) * jnp.exp(draft_max - d_max) / d_total
     t_factor = valid * jnp.exp(teach_max - t_max) / t_total
 
-    def grad_body(j, carry):
-        sl = pl.ds(pl.multiple_of(j * sb, sb), sb)
-        g[sl, :] = (d_factor * ed[sl, :] - t_factor * tl[sl, :] - valid * hit[sl, :]).astype(BF16)
-        return carry
-
-    lax.fori_loop(0, n // sb, grad_body, 0)
-
-    def back(o, to, which):
+    def back(o, to, which, first=False):
         @pl.when(v >= 0)
         def _():
+            rhs = g[...] if not first else (
+                d_factor * ed[...] - t_factor * tl[...] - valid * hit[...]
+            ).astype(BF16)
+            if first:
+                g[...] = rhs
             for b in which:
                 rows = pl.ds(b * f, f)
                 if not isinstance(b, int):
                     rows = pl.ds(pl.multiple_of(b * f, f), f)
-                part[o, b] = jnp.dot(head_v[to, rows, :], g[...], preferred_element_type=F32)
-
-    swaps = [
-        remote(part.at[o, 1 - c], sibp.at[o], rs_send.at[0], rs_recv.at[o], {"voc": sib})
-        for o in range(4)
+                part[o, b] = jnp.dot(head_v[to, rows, :], rhs, preferred_element_type=F32)
+
+    swaps = {
+        o: remote(part.at[o, 1 - c], sibp.at[o], rs_send.at[0], rs_recv.at[o], {"voc": sib})
+        for o in (0, 1, 3)
+    }
+    swap_far = remote(swap_two.at[0], swap_two.at[1], rs_send.at[3], rs_recv.at[2], {"voc": sib})
+
+    fq = f // 4
+    quads = [pl.ds(i * fq, fq) for i in range(4)]
+    flo, fhi = pl.ds(0, fh), pl.ds(fh, fh)
+    ways = (right, right, left, left)
+    out_two = [
+        remote(two.at[q], far.at[q], rs_send.at[1], rs_recv.at[4 + i], {"voc": ways[i]})
+        for i, q in enumerate(quads)
     ]
 
-    flo, fhi = pl.ds(0, fh), pl.ds(fh, fh)
-    out_two_r = remote(two.at[flo], far.at[flo], rs_send.at[1], rs_recv.at[4], {"voc": right})
-    out_two_l = remote(two.at[fhi], far.at[fhi], rs_send.at[1], rs_recv.at[5], {"voc": left})
-
     def out_near(i, h, to):
-        return remote(near.at[i, h], inn.at[i, h], rs_send.at[2], rs_recv.at[6], {"voc": to})
-
-    back(2, xo, (1 - c,))
-    swaps[2].start()
-    back(2, xo, (c,))
-    back(1, xr, (0, 1))
+        return remote(near.at[i, h], inn.at[i, h], rs_send.at[2], rs_recv.at[8], {"voc": to})
+
+
+    def far_sum(b):
+        rows = pl.ds(pl.multiple_of(b * f, f), f)
+        return d_factor * far_part[0, rows] - t_factor * far_part[1, rows] - valid * far_part[2, rows]
+
+    swap_two[0] = far_sum(1 - c).astype(BF16)
+    swap_far.start()
+    part[2, 0] = far_sum(c)
+    back(1, xr, (0, 1), True)
     swaps[1].start()
-    swaps[2].wait_recv()
-    two[...] = (part[2, c] + sibp[2]).astype(BF16)
-    out_two_r.start()
-    out_two_l.start()
+    swap_far.wait_recv()
+    two[...] = (part[2, 0] + swap_two[1].astype(F32)).astype(BF16)
+    for i in (0, 2, 1, 3):
+        out_two[i].start()
     back(3, xl, (0, 1))
     swaps[3].start()
     swaps[1].wait_recv()
@@ -397,26 +448,25 @@
     swaps[3].wait_recv()
     near[1, 0:fh, :] = (part[3, c, 0:fh, :] + sibp[3, 0:fh, :]).astype(BF16)
     out_near(1, flo, left).start()
-    out_two_r.wait_recv()
-    near[0, 0:fh, :] = (
-        part[1, c, 0:fh, :] + sibp[1, 0:fh, :] + far[0:fh, :].astype(F32)
-    ).astype(BF16)
-    out_near(0, flo, right).start()
-    out_two_l.wait_recv()
-    near[1, fh:f, :] = (
-        part[3, c, fh:f, :] + sibp[3, fh:f, :] + far[fh:f, :].astype(F32)
-    ).astype(BF16)
-    out_near(1, fhi, left).start()
+    for i in (0, 2, 1, 3):
+        out_two[i].wait_recv()
+        side, o = i // 2, 1 + i // 2 * 2
+        a, b = i * fq, (i + 1) * fq
+        near[side, a:b, :] = (
+            part[o, c, a:b, :] + sibp[o, a:b, :] + far[a:b, :].astype(F32)
+        ).astype(BF16)
+        out_near(side, quads[i], ways[i]).start()
     swaps[0].wait_recv()
     mine = part[0, c] + sibp[0]
-    both = remote(near, inn, rs_send.at[2], rs_recv.at[6], {"voc": sib})
+    both = remote(near, inn, rs_send.at[2], rs_recv.at[8], {"voc": sib})
     both.wait_recv()
     total = mine + inn[0].astype(F32) + inn[1].astype(F32)
     grad[...] = (loss_scale * total).T.astype(BF16)
 
-    all_swaps = remote(sibp, sibp, rs_send.at[0], rs_recv.at[0], {"voc": sib})
+    three = sibp.at[pl.ds(0, 3)]
+    all_swaps = remote(three, three, rs_send.at[0], rs_recv.at[0], {"voc": sib})
     all_two = remote(two, far, rs_send.at[1], rs_recv.at[4], {"voc": sib})
-    for cp in (d_all, t_all, all_packs, all_stats, all_swaps, all_two, both):
+    for cp in (d_all, t_all, early_wait(7, 0), swap_far, all_packs, all_stats, all_swaps, all_two, both):
         cp.wait_send()
 
 
@@ -453,18 +503,22 @@
             pltpu.VMEM((n, r), BF16),
             pltpu.VMEM((4, 2, f, r), F32),
             pltpu.VMEM((4, f, r), F32),
+            pltpu.VMEM((3, 2 * f, r), F32),
+            pltpu.VMEM((2, f, r), BF16),
             pltpu.VMEM((f, r), BF16),
             pltpu.VMEM((f, r), BF16),
             pltpu.VMEM((2, f, r), BF16),
             pltpu.VMEM((2, f, r), BF16),
             pltpu.VMEM((8, 8, r), F32),
+            pltpu.VMEM((8, r), F32),
             dma((10,)),
-            dma((2,)),
+            dma((3,)),
             dma((2, 6)),
             dma((2,)),
             dma((2,)),
-            dma((3,)),
-            dma((7,)),
+            dma((2,)),
+            dma((4,)),
+            dma((9,)),
         ],
         compiler_params=pltpu.CompilerParams(
             collective_id=0, has_side_effects=True, vmem_limit_bytes=56 * 1024 * 1024

time: 39.4 us -> 37.2 us (0.944)
  Pallas kernels: 37.3 us -> 35.2 us
    pallas_call x1, Pallas kernels: 37.3 us -> 35.2 us  [per_device(): pl.pallas_call(functools.partial(kernel, n_tok), out_shape=(pltpu.VMEM((1...]
where the time goes in v3:
time: 37.2 us; the launch traced here: 37.1 us
  Pallas kernels  35.2 us (95%)
  local copies, waits for them, and re-layouts  1.22 us (3%)
  between operations  0.64 us (2%)
    pallas_call x1, Pallas kernels, per_device(): pl.pallas_call(functools.partial(kernel, n_tok), out_shape=(pltpu.VMEM((1...  35.2 us
    unnamed x2, local copies, waits for them, and re-layouts  1.22 us

profile of v3, /device:TPU:1, one launch (start us, length us, event | category | flops | bytes accessed | tf_op | source)
XLA Modules:
  0.0 37.1 jit_solution(13290400547426205633)
XLA Ops:
  0.6 35.2 %shard_map.86 = (f32[1,256]{1,0:T(1,128)S(1)}, bf16[256,256]{1,0:T(8,128)(2,1)S(1)}) custom-call(bf16[256,256]{1,0:T(8,128)(2,1)} %teach.1, bf16[256,256]{1,0:T(8,128)(2,1)} %draft.1, bf16[2048,2048]{1,0:T(8,128)(2,1)} %head.1, s32[1,2048]{1,0:T(1,128)} %bitcast.5, s32[1,256]{1,0:T(1,128)} %bitcast.6, s32[1,256]{1,0:T(1,128)} %bitcast.7, s32[32]{0:T(128)} %counts_hbm.1), custom_call_target="tpu_custom_call" | custom-call | tf_op jit(solution)/shard_map/pallas_call | solution.py:479
  35.9 0.6 %copy.11 = f32[256]{0:T(256)} copy(f32[256]{0:T(256)S(1)} %bitcast.4) | data formatting | bytes 2048
  36.4 0.7 %copy.12 = bf16[256,256]{1,0:T(8,128)(2,1)} copy(bf16[256,256]{1,0:T(8,128)(2,1)S(1)} %get-tuple-element.7) | data formatting | bytes 262144

commit v4 on v3

--- a/solution.py
+++ b/solution.py
@@ -269,23 +269,23 @@
     multiply(dl, rows_d, (v, sib, left, right), True)
     t_send[2].start()
     t_send[4].start()
-
-    @pl.when(v >= 0)
-    def _():
-        ones = hit[...].astype(BF16)
-        far_part[2] = jnp.dot(head_v[xo], ones, preferred_element_type=F32)
-
     d_recv[3].wait_recv()
     d_send[9].start()
     d_send[10].start()
-    early_wait(3, 0).wait_recv()
-    for cp in early_pass:
-        cp.start()
     d_recv[4].wait_recv()
     multiply(dl, rows_d, (left_s, right_s), False)
     t_recv[1].wait_recv()
     t_send[5].start()
     t_send[6].start()
+    early_wait(3, 0).wait_recv()
+    for cp in early_pass:
+        cp.start()
+
+    @pl.when(v >= 0)
+    def _():
+        ones = hit[...].astype(BF16)
+        far_part[2] = jnp.dot(head_v[xo], ones, preferred_element_type=F32)
+
     d_recv[5].wait_recv()
     multiply(dl, rows_d, (opp, opp_s), False, True)
     draft_max = jnp.max(top[...], axis=0, keepdims=True)

time: 37.2 us -> 37.2 us (level)
  no operation moved by 1% of the time
where the time goes in v4:
time: 37.2 us; the launch traced here: 37.1 us
  Pallas kernels  35.2 us (95%)
  local copies, waits for them, and re-layouts  1.22 us (3%)
  between operations  0.64 us (2%)
    pallas_call x1, Pallas kernels, per_device(): pl.pallas_call(functools.partial(kernel, n_tok), out_shape=(pltpu.VMEM((1...  35.2 us
    unnamed x2, local copies, waits for them, and re-layouts  1.22 us

profile of v4, /device:TPU:1, one launch (start us, length us, event | category | flops | bytes accessed | tf_op | source)
XLA Modules:
  0.0 37.1 jit_solution(11311131915603771585)
XLA Ops:
  0.6 35.2 %shard_map.86 = (f32[1,256]{1,0:T(1,128)S(1)}, bf16[256,256]{1,0:T(8,128)(2,1)S(1)}) custom-call(bf16[256,256]{1,0:T(8,128)(2,1)} %teach.1, bf16[256,256]{1,0:T(8,128)(2,1)} %draft.1, bf16[2048,2048]{1,0:T(8,128)(2,1)} %head.1, s32[1,2048]{1,0:T(1,128)} %bitcast.5, s32[1,256]{1,0:T(1,128)} %bitcast.6, s32[1,256]{1,0:T(1,128)} %bitcast.7, s32[32]{0:T(128)} %counts_hbm.1), custom_call_target="tpu_custom_call" | custom-call | tf_op jit(solution)/shard_map/pallas_call | solution.py:479
  35.9 0.6 %copy.11 = f32[256]{0:T(256)} copy(f32[256]{0:T(256)S(1)} %bitcast.4) | data formatting | bytes 2048
  36.4 0.7 %copy.12 = bf16[256,256]{1,0:T(8,128)(2,1)} copy(bf16[256,256]{1,0:T(8,128)(2,1)S(1)} %get-tuple-element.7) | data formatting | bytes 262144

commit v5 on v4

--- a/solution.py
+++ b/solution.py
@@ -392,7 +392,7 @@
     d_factor = valid * (1.0 + hits) * jnp.exp(draft_max - d_max) / d_total
     t_factor = valid * jnp.exp(teach_max - t_max) / t_total
 
-    def back(o, to, which, first=False):
+    def back(slices, first=False):
         @pl.when(v >= 0)
         def _():
             rhs = g[...] if not first else (
@@ -400,16 +400,21 @@
             ).astype(BF16)
             if first:
                 g[...] = rhs
-            for b in which:
-                rows = pl.ds(b * f, f)
-                if not isinstance(b, int):
-                    rows = pl.ds(pl.multiple_of(b * f, f), f)
-                part[o, b] = jnp.dot(head_v[to, rows, :], rhs, preferred_element_type=F32)
-
-    swaps = {
-        o: remote(part.at[o, 1 - c], sibp.at[o], rs_send.at[0], rs_recv.at[o], {"voc": sib})
-        for o in (0, 1, 3)
-    }
+            for o, to, a, b in slices:
+                for i in range(2):
+                    part[o, i, a:b] = jnp.dot(
+                        head_v[to, i * f + a : i * f + b, :], rhs, preferred_element_type=F32
+                    )
+
+    def swap(o, a, b, sem):
+        rows = pl.ds(a, b - a)
+        return remote(
+            part.at[o, 1 - c, rows], sibp.at[o, rows], rs_send.at[0], rs_recv.at[sem], {"voc": sib}
+        )
+
+    swap_r, swap_l = swap(1, fh, f, 1), swap(3, 0, fh, 3)
+    swap_rest = [swap(1, 0, fh, 9), swap(3, fh, f, 9)]
+    swap_own = swap(0, 0, f, 0)
     swap_far = remote(swap_two.at[0], swap_two.at[1], rs_send.at[3], rs_recv.at[2], {"voc": sib})
 
     fq = f // 4
@@ -432,22 +437,25 @@
     swap_two[0] = far_sum(1 - c).astype(BF16)
     swap_far.start()
     part[2, 0] = far_sum(c)
-    back(1, xr, (0, 1), True)
-    swaps[1].start()
+    back(((1, xr, fh, f), (3, xl, 0, fh)), True)
+    swap_r.start()
+    swap_l.start()
     swap_far.wait_recv()
     two[...] = (part[2, 0] + swap_two[1].astype(F32)).astype(BF16)
     for i in (0, 2, 1, 3):
         out_two[i].start()
-    back(3, xl, (0, 1))
-    swaps[3].start()
-    swaps[1].wait_recv()
+    back(((1, xr, 0, fh), (3, xl, fh, f)))
+    for cp in swap_rest:
+        cp.start()
+    swap_r.wait_recv()
     near[0, fh:f, :] = (part[1, c, fh:f, :] + sibp[1, fh:f, :]).astype(BF16)
     out_near(0, fhi, right).start()
-    back(0, x, (0, 1))
-    swaps[0].start()
-    swaps[3].wait_recv()
+    swap_l.wait_recv()
     near[1, 0:fh, :] = (part[3, c, 0:fh, :] + sibp[3, 0:fh, :]).astype(BF16)
     out_near(1, flo, left).start()
+    back(((0, x, 0, f),))
+    swap_own.start()
+    remote(sibp.at[0], sibp.at[0], rs_send.at[0], rs_recv.at[9], {"voc": sib}).wait_recv()
     for i in (0, 2, 1, 3):
         out_two[i].wait_recv()
         side, o = i // 2, 1 + i // 2 * 2
@@ -456,7 +464,7 @@
             part[o, c, a:b, :] + sibp[o, a:b, :] + far[a:b, :].astype(F32)
         ).astype(BF16)
         out_near(side, quads[i], ways[i]).start()
-    swaps[0].wait_recv()
+    swap_own.wait_recv()
     mine = part[0, c] + sibp[0]
     both = remote(near, inn, rs_send.at[2], rs_recv.at[8], {"voc": sib})
     both.wait_recv()
@@ -518,7 +526,7 @@
             dma((2,)),
             dma((2,)),
             dma((4,)),
-            dma((9,)),
+            dma((10,)),
         ],
         compiler_params=pltpu.CompilerParams(
             collective_id=0, has_side_effects=True, vmem_limit_bytes=56 * 1024 * 1024

time: 37.2 us -> 37.2 us (level)
  no operation moved by 1% of the time
where the time goes in v5:
time: 37.2 us; the launch traced here: 37.1 us
  Pallas kernels  35.2 us (95%)
  local copies, waits for them, and re-layouts  1.22 us (3%)
  between operations  0.64 us (2%)
    pallas_call x1, Pallas kernels, per_device(): pl.pallas_call(functools.partial(kernel, n_tok), out_shape=(pltpu.VMEM((1...  35.2 us
    unnamed x2, local copies, waits for them, and re-layouts  1.22 us

profile of v5, /device:TPU:1, one launch (start us, length us, event | category | flops | bytes accessed | tf_op | source)
XLA Modules:
  0.0 37.1 jit_solution(2687217898225993443)
XLA Ops:
  0.6 35.2 %shard_map.86 = (f32[1,256]{1,0:T(1,128)S(1)}, bf16[256,256]{1,0:T(8,128)(2,1)S(1)}) custom-call(bf16[256,256]{1,0:T(8,128)(2,1)} %teach.1, bf16[256,256]{1,0:T(8,128)(2,1)} %draft.1, bf16[2048,2048]{1,0:T(8,128)(2,1)} %head.1, s32[1,2048]{1,0:T(1,128)} %bitcast.5, s32[1,256]{1,0:T(1,128)} %bitcast.6, s32[1,256]{1,0:T(1,128)} %bitcast.7, s32[32]{0:T(128)} %counts_hbm.1), custom_call_target="tpu_custom_call" | custom-call | tf_op jit(solution)/shard_map/pallas_call | solution.py:487
  35.9 0.6 %copy.11 = f32[256]{0:T(256)} copy(f32[256]{0:T(256)S(1)} %bitcast.4) | data formatting | bytes 2048
  36.4 0.7 %copy.12 = bf16[256,256]{1,0:T(8,128)(2,1)} copy(bf16[256,256]{1,0:T(8,128)(2,1)S(1)} %get-tuple-element.7) | data formatting | bytes 262144

commit v6 on v4

--- a/solution.py
+++ b/solution.py
@@ -195,6 +195,27 @@
     for i in (1, 3, 0):
         d_send[i].start()
 
+    def turn(i):
+        load_h[i].wait()
+        for b in range(2):
+            for j in range(n // 256):
+                head_t[2 * i + b, j * 256 : (j + 1) * 256, :] = head_v[
+                    i, b * f : (b + 1) * f, j * 256 : (j + 1) * 256
+                ].T
+
+    all_packs = remote(
+        pack.at[pl.ds(1, 3)], got.at[pl.ds(1, 3)], pk_sem.at[0], pk_sem.at[1], {"voc": sib}
+    )
+    turn(0)
+    d_send[2].start()
+    d_send[4].start()
+    turn(1)
+    for cp in early_near:
+        cp.start()
+    d_recv[1].wait_recv()
+    d_send[5].start()
+    d_send[6].start()
+    early_far.start()
     for cp in load_s[1:]:
         cp.wait()
     targets = targ[...].astype(F32)
@@ -208,28 +229,7 @@
         hits_sum = hits_sum + jnp.sum(h.reshape(16, 8, r), axis=0)
     local_hits = jnp.sum(hits_sum, axis=0, keepdims=True)
 
-    def turn(i):
-        load_h[i].wait()
-        for b in range(2):
-            for j in range(n // 256):
-                head_t[2 * i + b, j * 256 : (j + 1) * 256, :] = head_v[
-                    i, b * f : (b + 1) * f, j * 256 : (j + 1) * 256
-                ].T
-
-    all_packs = remote(
-        pack.at[pl.ds(1, 3)], got.at[pl.ds(1, 3)], pk_sem.at[0], pk_sem.at[1], {"voc": sib}
-    )
-    turn(0)
-    d_send[2].start()
-    d_send[4].start()
-    turn(1)
     turn(2)
-    for cp in early_near:
-        cp.start()
-    d_recv[1].wait_recv()
-    d_send[5].start()
-    d_send[6].start()
-    early_far.start()
     turn(3)
     d_recv[2].wait_recv()
     d_send[7].start()

time: 37.2 us -> 37.2 us (level)
  no operation moved by 1% of the time
where the time goes in v6:
time: 37.2 us; the launch traced here: 37.1 us
  Pallas kernels  35.2 us (95%)
  local copies, waits for them, and re-layouts  1.22 us (3%)
  between operations  0.64 us (2%)
    pallas_call x1, Pallas kernels, per_device(): pl.pallas_call(functools.partial(kernel, n_tok), out_shape=(pltpu.VMEM((1...  35.2 us
    unnamed x2, local copies, waits for them, and re-layouts  1.22 us

profile of v6, /device:TPU:1, one launch (start us, length us, event | category | flops | bytes accessed | tf_op | source)
XLA Modules:
  0.0 37.1 jit_solution(6001735721526026394)
XLA Ops:
  0.6 35.2 %shard_map.86 = (f32[1,256]{1,0:T(1,128)S(1)}, bf16[256,256]{1,0:T(8,128)(2,1)S(1)}) custom-call(bf16[256,256]{1,0:T(8,128)(2,1)} %teach.1, bf16[256,256]{1,0:T(8,128)(2,1)} %draft.1, bf16[2048,2048]{1,0:T(8,128)(2,1)} %head.1, s32[1,2048]{1,0:T(1,128)} %bitcast.5, s32[1,256]{1,0:T(1,128)} %bitcast.6, s32[1,256]{1,0:T(1,128)} %bitcast.7, s32[32]{0:T(128)} %counts_hbm.1), custom_call_target="tpu_custom_call" | custom-call | tf_op jit(solution)/shard_map/pallas_call | solution.py:479
  35.9 0.6 %copy.11 = f32[256]{0:T(256)} copy(f32[256]{0:T(256)S(1)} %bitcast.4) | data formatting | bytes 2048
  36.4 0.7 %copy.12 = bf16[256,256]{1,0:T(8,128)(2,1)} copy(bf16[256,256]{1,0:T(8,128)(2,1)S(1)} %get-tuple-element.7) | data formatting | bytes 262144
